TPU v7x, 256 devices: a whole 4x4x8 slice. The times are simulated.
256 devices in a mesh: segment: 2 (over core), rows: 32 (over z, x), dp: 4 (over y).
Axes of the slice: x: 4, y: 4, z: 8, core: 2. Of those that a mesh axis runs over, the one named last changes fastest.
Arguments:
- coarse: bfloat16 [8, 100, 384, 256], P(('segment', 'dp'), None, 'rows'), may hold values from -6 to 6
- target: bfloat16 [8, 64, 384, 256], P(('segment', 'dp'), None, 'rows'), may hold values from -6 to 6
- noise: bfloat16 [8, 32, 64, 64, 144], P(('segment', 'dp'), 'rows'), may hold values from -6 to 6
- regions: int32 [8, 32, 32, 4], P(('segment', 'dp')), may hold values from 0 to 244, as said below
- reg_conv: bfloat16 [128, 900], replicated, may hold values from -0.1875 to 0.1875
- reg_out: bfloat16 [64, 128], replicated, may hold values from -0.5 to 0.5
- conv_one: bfloat16 [128, 1152], replicated, may hold values from -0.1875 to 0.1875
- conv_two: bfloat16 [128, 1152], replicated, may hold values from -0.1875 to 0.1875
- out_proj: bfloat16 [64, 128], replicated, may hold values from -0.5 to 0.5
- step_embed: float32 [32, 128], replicated, may hold values from -3 to 3
Outputs:
- mean_field: bfloat16 [8, 64, 384, 256], P(('segment', 'dp'), None, 'rows')
- owner_loss: float32 [8, 32], P(('segment', 'dp'), 'rows')
- grad_conv_one: float32 [128, 1152], replicated
- grad_conv_two: float32 [128, 1152], replicated
- grad_out_proj: float32 [64, 128], replicated
- grad_embed: float32 [32, 128], replicated
Inputs may be any that keep to these rules, and one draw needn't show every extreme that they name: `regions`: for sample s, strip i and entry k: entry 0 is the patch's row offset within strip i (0 on the last strip), entry 1 its first column, at most 244, entry 2 its owner, entry 3 its noise level below 32. Every owner receives 2 * 32, 32 or 16 patches of a sample; for each owner with 64 there is one with 32 and two with 16. No strip lists more than 2 patches for one owner, and some strip lists exactly 2 for one owner.
All inputs are finite; a program needn't handle non-finite values.
Results may differ from a plain program's by a relative error of at most 0.0048.
Values may be sent and summed in bfloat16 or wider, within the bound.
A program may use at most 192 MiB of HBM per device.

v0:
```python
import math
import jax
import jax.numpy as jnp
from jax import lax
from jax.sharding import PartitionSpec as P

PATCH = 12
TAPS = ((-1, -1), (-1, 0), (-1, 1), (0, -1), (0, 0), (0, 1), (1, -1), (1, 0), (1, 1))


def padded_2(cells, sides, width):
    for axis, dim in sides:
        count = lax.axis_size(axis)
        ends = count - 1
        head = lax.slice_in_dim(cells, 0, width, axis=dim)
        tail = lax.slice_in_dim(cells, cells.shape[dim] - width, cells.shape[dim], axis=dim)
        cells = jnp.concatenate(
            [
                lax.ppermute(tail, axis, [(i, (i + 1) % count) for i in range(ends)]),
                cells,
                lax.ppermute(head, axis, [((i + 1) % count, i) for i in range(ends)]),
            ],
            axis=dim,
        )
    return cells


def shifted_2(block, axis, distance):
    devices = range(lax.axis_size(axis))
    route = [(i - distance, i) for i in devices if i - distance in devices]
    return lax.ppermute(block, axis, route)


def shifted(values, row_step, col_step, stride):
    length = values.shape[-1]
    margin = stride + 1
    widths = [(0, 0)] * (values.ndim - 1) + [(margin, margin)]
    padded = jnp.pad(values, widths)
    offset = margin + row_step * stride + col_step
    moved = lax.slice_in_dim(padded, offset, offset + length, axis=values.ndim - 1)
    column = jnp.arange(length, dtype=jnp.int32) % stride + col_step
    inside = (column >= 0) & (column < stride)
    return jnp.where(inside, moved, jnp.zeros((), moved.dtype))


def columns(values, stride):
    return jnp.concatenate(
        [shifted(values, row_step, col_step, stride) for row_step, col_step in TAPS], axis=-2
    )


def fold(gradients, stride):
    width = gradients.shape[-2] // 9
    result = jnp.zeros(gradients.shape[:-2] + (width, gradients.shape[-1]), jnp.float32)
    for position, (row_step, col_step) in enumerate(TAPS):
        piece = gradients[..., position * width : (position + 1) * width, :]
        result = result + shifted(piece, -row_step, -col_step, stride)
    return result


def noise_levels(level_count):
    steps_f = jnp.arange(level_count, dtype=jnp.float32)
    return 0.1 * jnp.exp(steps_f * (math.log(100.0) / (level_count - 1)))


def silu_slope(values):
    gate = jax.nn.sigmoid(values)
    return gate * (1.0 + values * (1.0 - gate))


def product(form, left, right):
    return jnp.einsum(form, left, right, preferred_element_type=jnp.float32)


def regress(grid_rows, reg_conv, reg_out):
    channels, height, width = grid_rows.shape
    flat = grid_rows.reshape(channels, height * width)
    hidden = product("ok,kp->op", reg_conv, columns(flat, width))
    activated = jax.nn.silu(hidden).astype(jnp.bfloat16)
    mean_flat = product("co,op->cp", reg_out, activated).astype(jnp.bfloat16)
    return mean_flat.reshape(reg_out.shape[0], height, width)


def patch_block(mean_part, target_part, noise_part, step_ids, in_use, weights):
    conv_one, conv_two, out_proj, step_embed = weights
    stride = PATCH
    level_count = step_embed.shape[0]
    sigma_table = noise_levels(level_count)
    step_hot = (step_ids[:, None] == jnp.arange(level_count, dtype=jnp.int32)[None, :]).astype(
        jnp.float32
    )
    sigma = jnp.sum(step_hot * sigma_table[None, :], axis=1)
    sigma_sq = sigma * sigma + 1.0
    scale_in = (1.0 / jnp.sqrt(sigma_sq))[:, None, None]
    scale_skip = (1.0 / sigma_sq)[:, None, None]
    scale_out = (sigma / jnp.sqrt(sigma_sq))[:, None, None]
    weight_loss = sigma_sq / (sigma * sigma)
    mean_float = mean_part.astype(jnp.float32)
    residual = target_part.astype(jnp.float32) - mean_float
    noisy = residual + sigma[:, None, None] * noise_part.astype(jnp.float32)
    inputs = jnp.concatenate([scale_in * noisy, mean_float], axis=1).astype(jnp.bfloat16)
    cols_in = columns(inputs, stride)
    embedded = jnp.sum(step_hot[:, :, None] * step_embed[None, :, :], axis=1)
    pre_one = product("ok,bkp->bop", conv_one, cols_in) + embedded[:, :, None]
    act_one = jax.nn.silu(pre_one).astype(jnp.bfloat16)
    cols_one = columns(act_one, stride)
    pre_two = product("ok,bkp->bop", conv_two, cols_one)
    act_two = jax.nn.silu(pre_two).astype(jnp.bfloat16)
    output = product("co,bop->bcp", out_proj, act_two)
    error = scale_skip * noisy + scale_out * output - residual
    losses = weight_loss * jnp.mean(error * error, axis=(1, 2)) * in_use
    factor = 2.0 * weight_loss * in_use / (error.shape[1] * error.shape[2])
    grad_output = (factor[:, None, None] * scale_out * error).astype(jnp.bfloat16)
    grad_proj = product("bcp,bop->co", grad_output, act_two)
    grad_act_two = product("co,bcp->bop", out_proj, grad_output)
    grad_pre_two = (grad_act_two * silu_slope(pre_two)).astype(jnp.bfloat16)
    grad_two = product("bop,bkp->ok", grad_pre_two, cols_one)
    grad_cols = product("ok,bop->bkp", conv_two, grad_pre_two)
    grad_act_one = fold(grad_cols, stride)
    grad_pre_one = (grad_act_one * silu_slope(pre_one)).astype(jnp.bfloat16)
    grad_one = product("bop,bkp->ok", grad_pre_one, cols_in)
    pixel_sums = jnp.sum(grad_pre_one, axis=2, dtype=jnp.float32)
    grad_table = jnp.sum(step_hot[:, :, None] * pixel_sums[:, None, :], axis=0)
    return (losses, (grad_one, grad_two, grad_proj, grad_table))


def run_blocks(mean_part, target_part, noise_part, step_ids, in_use, weights):
    patch_count = mean_part.shape[0]
    blocks = patch_count // 4

    def regroup(values):
        return values.reshape((blocks, 4) + values.shape[1:])

    def advance(running, group_block):
        losses, gradients = patch_block(
            group_block[0], group_block[1], group_block[2], group_block[3], group_block[4], weights
        )
        summed = (
            running[0] + gradients[0],
            running[1] + gradients[1],
            running[2] + gradients[2],
            running[3] + gradients[3],
        )
        return (summed, losses)

    initial = (
        jnp.zeros(weights[0].shape, jnp.float32),
        jnp.zeros(weights[1].shape, jnp.float32),
        jnp.zeros(weights[2].shape, jnp.float32),
        jnp.zeros(weights[3].shape, jnp.float32),
    )
    stacked = (
        regroup(mean_part),
        regroup(target_part),
        regroup(noise_part),
        regroup(step_ids),
        regroup(in_use),
    )
    gradients, losses = lax.scan(advance, initial, stacked)
    return (losses.reshape(patch_count), gradients)


def owner_tables(region_rows, strips):
    owners = region_rows[:, :, 2]
    owner_hot = (owners[:, :, None] == jnp.arange(strips, dtype=jnp.int32)[None, None, :]).astype(
        jnp.int32
    )
    pair_rank = jnp.sum((jnp.cumsum(owner_hot, axis=1) - owner_hot) * owner_hot, axis=2)
    flat_hot = owner_hot.reshape(-1, strips)
    owner_slot = jnp.sum((jnp.cumsum(flat_hot, axis=0) - flat_hot) * flat_hot, axis=1).reshape(
        owners.shape
    )
    return (owners, pair_rank, owner_slot)


def owned_slots(region_rows, owners, pair_rank, owner_slot, strip_index, capacity, most, height):
    strips = region_rows.shape[0]
    slot_hits = (
        (owners == strip_index)[:, :, None]
        & (owner_slot[:, :, None] == jnp.arange(most, dtype=jnp.int32)[None, None, :])
    ).astype(jnp.int32)
    strip_ids = jnp.arange(strips, dtype=jnp.int32)[:, None]
    recv_index = jnp.sum(slot_hits * (strip_ids * capacity + pair_rank)[:, :, None], axis=(0, 1))
    in_use = jnp.sum(slot_hits, axis=(0, 1)).astype(jnp.float32)
    step_ids = jnp.sum(slot_hits * region_rows[:, :, 3][:, :, None], axis=(0, 1))
    row_at = jnp.sum(
        slot_hits * (strip_ids * height + region_rows[:, :, 0])[:, :, None], axis=(0, 1)
    )
    col_at = jnp.sum(slot_hits * region_rows[:, :, 1][:, :, None], axis=(0, 1))
    return (recv_index, in_use, step_ids, row_at, col_at)


def cut_patches(source_grid, row_at, col_at, height):
    zero_index = jnp.zeros((), jnp.int32)

    def cut(row_start, col_start):
        piece = lax.dynamic_slice(
            source_grid,
            (zero_index, zero_index, row_start, col_start),
            (2, source_grid.shape[1], height, height),
        )
        return piece.reshape(2, source_grid.shape[1], height * height)

    return jax.vmap(cut)(row_at, col_at)


def per_device(
    coarse, target, noise, regions, reg_conv, reg_out, conv_one, conv_two, out_proj, step_embed
):
    strips = lax.axis_size("rows")
    strip_index = lax.axis_index("rows")
    region_rows = regions[0]
    per_strip = region_rows.shape[1]
    capacity = max(2, (2 * per_strip + strips - 1) // strips)
    most = 2 * per_strip
    weights = (conv_one, conv_two, out_proj, step_embed)
    rimmed = padded_2(coarse, (("rows", 2),), 1)
    mean_strip = regress(rimmed[0], reg_conv, reg_out)[:, 1:-1]
    height = mean_strip.shape[1]
    pair_strip = jnp.stack([mean_strip, target[0]])
    owners, pair_rank, owner_slot = owner_tables(region_rows, strips)
    own_regions = lax.dynamic_index_in_dim(region_rows, strip_index, 0, keepdims=False)
    own_pairs = lax.dynamic_index_in_dim(pair_rank, strip_index, 0, keepdims=False)
    slot_noise = noise[0, 0]
    below = shifted_2(pair_strip[:, :, : height - 1], "rows", -1)
    extended = jnp.concatenate([pair_strip, below], axis=2)
    patches = cut_patches(extended, own_regions[:, 0], own_regions[:, 1], height)
    outgoing = jnp.zeros((strips, capacity) + patches.shape[1:], patches.dtype)
    outgoing = outgoing.at[own_regions[:, 2], own_pairs].set(patches)
    received = lax.all_to_all(outgoing, "rows", split_axis=0, concat_axis=0, tiled=True)
    flat_recv = received.reshape((strips * capacity,) + patches.shape[1:])
    recv_index, in_use, step_ids, row_at, col_at = owned_slots(
        region_rows, owners, pair_rank, owner_slot, strip_index, capacity, most, height
    )
    gathered = jnp.take(flat_recv, recv_index, axis=0)
    losses, gradients = run_blocks(
        gathered[:, 0], gathered[:, 1], slot_noise, step_ids, in_use, weights
    )
    owner_total = jnp.sum(losses)
    totals = lax.psum(
        (gradients[0], gradients[1], gradients[2], gradients[3]), ("segment", "rows", "dp")
    )
    return (mean_strip[None], owner_total.reshape(1, 1), totals[0], totals[1], totals[2], totals[3])


def solution(mesh):
    placed = (
        P(("segment", "dp"), None, "rows", None),
        P(("segment", "dp"), None, "rows", None),
        P(("segment", "dp"), "rows", None, None, None),
        P(("segment", "dp"), None, None, None),
        P(),
        P(),
        P(),
        P(),
        P(),
        P(),
    )
    return jax.shard_map(
        per_device,
        mesh=mesh,
        in_specs=placed,
        out_specs=(
            P(("segment", "dp"), None, "rows", None),
            P(("segment", "dp"), "rows"),
            P(),
            P(),
            P(),
            P(),
        ),
        check_vma=False,
    )
```

profile of v0, /device:TPU:8, one launch (start us, length us, event | category | flops | bytes accessed | tf_op | source)
XLA Modules:
  0.0 851.5 jit_solution(5382771631686754666)
XLA Ops:
  8.1 3.4 collective-permute-start
  12.8 3.2 copy.114
  18.2 4.4 slice_select_fusion.1
  22.6 41.7 %concatenate.38 = bf16[900,3584]{1,0:T(8,128)(2,1)} concatenate(bf16[100,3584]{1,0:T(8,128)(2,1)} %get-tuple-element.387, bf16[100,3584]{1,0:T(8,128)(2,1)} %get-tuple-element.390, bf16[100,3584]{1,0:T(8,128)(2,1)} %get-tuple-element.380, bf16[100,3584]{1,0:T(8,128)(2,1)} %get-tuple-element.388, bf16[100,3584]{1,0:T(8,128)(2,1)} %get-tuple-element.391, ...), dimensions={0} | concatenate | bytes 12902400 | tf_op jit(solution)/shard_map/concatenate | solution.py:47
  64.3 5.4 fusion.29
  71.2 3.2 copy.113
  74.4 4.9 pad_maximum_fusion.2
  79.3 4.6 copy.115
  87.4 16.4 %collective-permute-done.2 = bf16[2,64,11,256]{3,1,2,0:T(8,128)(2,1)} collective-permute-done((bf16[2,64,11,256]{3,1,2,0:T(8,128)(2,1)}, bf16[2,64,11,256]{3,1,2,0:T(8,128)(2,1)}, u32[]{:S(2)}, u32[]{:S(2)}) %collective-permute-start.2) | collective-permute-done | bytes 720928 | tf_op jit(solution)/shard_map/ppermute | solution.py:31
  103.8 4.7 copy.116
  108.4 8.1 pad_maximum_fusion.1
  116.5 8.6 %gather_fusion = bf16[32,2,64,12,12]{2,1,4,3,0:T(2,128)(2,1)S(1)} fusion(bf16[2,64,23,256]{1,0,3,2:T(2,128)(2,1)} %pad_maximum_fusion.1, s32[32]{0:T(128)S(1)} %get-tuple-element.398), kind=kCustom, calls=%fused_computation | custom fusion | bytes 2359808 | tf_op jit(solution)/shard_map/vmap()/gather | solution.py:197
  125.2 3.9 copy.117
  131.6 5.7 scatter_fusion
  137.3 15.6 %all-to-all-start = ((bf16[32,2,2,64,144]{4,3,2,1,0:T(8,128)(2,1)}), bf16[32,2,2,64,144]{4,3,2,1,0:T(8,128)(2,1)}, u32[]{:S(2)}, u32[]{:S(2)}) async-start(bf16[32,2,2,64,144]{4,3,2,1,0:T(8,128)(2,1)} %scatter_fusion), calls=%async_computation | async-start | bytes 8388608 | tf_op jit(solution)/shard_map/all_to_all | solution.py:230
  153.4 9.0 %reduce-window.6 = s32[32,8,128]{2,1,0:T(8,128)S(1)} reduce-window(s32[32,8,128]{2,1,0:T(8,128)S(1)} %fusion.38, s32[]{:T(128)} %constant.269.clone.1), window={size=1x1x128 pad=0_0x0_0x127_0}, to_apply=%region_0.1 | reduce-window | flops 4161536 | bytes 262148 | tf_op jit(solution)/shard_map/reduce-window
  164.0 81.0 %all-to-all-done = bf16[32,2,2,64,144]{4,3,2,1,0:T(8,128)(2,1)} async-done(((bf16[32,2,2,64,144]{4,3,2,1,0:T(8,128)(2,1)}), bf16[32,2,2,64,144]{4,3,2,1,0:T(8,128)(2,1)}, u32[]{:S(2)}, u32[]{:S(2)}) %all-to-all-start) | async-done | bytes 2359328 | tf_op jit(solution)/shard_map/all_to_all | solution.py:230
  245.0 5.0 gather_fusion.1
  255.2 328.0 %while.21 = (s32[]{:T(128)}, f32[128,1152]{1,0:T(8,128)}, f32[128,1152]{1,0:T(8,128)}, f32[64,128]{1,0:T(8,128)S(1)}, f32[32,128]{1,0:T(8,128)S(1)}, /*index=5*/...) while((s32[]{:T(128)}, f32[128,1152]{1,0:T(8,128)}, ...), condition=%wide.region_15.16_spmd.clone, body=%wide.region_9.15_spmd.clone.sunk | while | flops 884677568 | bytes 48410204 | solution.py:159
  286.9 2.8 fusion.117
  307.5 2.8 fusion.117
  328.0 2.8 fusion.117
  348.6 2.8 fusion.117
  369.2 2.8 fusion.117
  410.3 2.8 fusion.117
  430.9 2.8 fusion.117
  472.0 2.8 fusion.117
  492.5 2.8 fusion.117
  533.7 2.8 fusion.117
  554.2 2.8 fusion.117
  584.5 74.9 %all-reduce.11 = (f32[64,128]{1,0:T(8,128)}, f32[32,128]{1,0:T(8,128)}) all-reduce(f32[64,128]{1,0:T(8,128)S(1)} %get-tuple-element.201, f32[32,128]{1,0:T(8,128)S(1)} %get-tuple-element.202), channel_id=1, replica_groups=mesh['segment'=2,'rows'=32,'dp'=4] {'segment','rows','dp'}, use_global_device_ids=true, to_apply=%region_19.20 | all-reduce | flops 12288 | bytes 98304 | tf_op jit(solution)/shard_map/psum | solution.py:240
  659.4 181.4 %all-reduce.15.cloned.1.call-done = (f32[128,1152]{1,0:T(8,128)}, f32[128,1152]{1,0:T(8,128)}) async-done(((f32[128,1152]{1,0:T(8,128)}, f32[128,1152]{1,0:T(8,128)}), (f32[128,1152]{1,0:T(8,128)}, f32[128,1152]{1,0:T(8,128)})) %all-reduce.15.cloned.1.call-update) | async-done | bytes 1179664 | tf_op jit(solution)/shard_map/psum | solution.py:240
  (909 shorter events, 317.0 us)
Async XLA Ops:
  7.2 57.2 %copy-start = (bf16[128,900]{0,1:T(8,128)(2,1)S(1)}, bf16[128,900]{0,1:T(8,128)(2,1)}, u32[]{:S(2)}) copy-start(bf16[128,900]{0,1:T(8,128)(2,1)} %param.16) | copy-start | bytes 691204
  7.2 10.4 %copy-start.9 = (bf16[1,100,12,256]{3,1,2,0:T(8,128)(2,1)S(1)}, bf16[1,100,12,256]{3,1,2,0:T(8,128)(2,1)}, u32[]{:S(2)}) copy-start(bf16[1,100,12,256]{3,1,2,0:T(8,128)(2,1)} %param.12) | copy-start | bytes 1843204
  8.1 8.8 %collective-permute-start = (bf16[1,100,1,256]{3,1,2,0:T(8,128)(2,1)S(1)}, bf16[1,100,1,256]{3,1,2,0:T(8,128)(2,1)S(1)}, u32[]{:S(2)}, u32[]{:S(2)}) collective-permute-start(bf16[1,100,1,256]{3,1,2,0:T(8,128)(2,1)S(1)} %get-tuple-element.393), channel_id=1, source_target_pairs={{0,4},{4,8},{8,12},{12,16},{16,20},{20,24},{24,28},{28,32},{32,36}... | collective-permute-start | bytes 153608 | tf_op jit(solution)/shard_map/ppermute | solution.py:19
  11.5 6.0 collective-permute-start.1
  22.6 41.7 %copy-start.12 = (bf16[64,128]{1,0:T(8,128)(2,1)S(1)}, bf16[64,128]{1,0:T(8,128)(2,1)}, u32[]{:S(2)}) copy-start(bf16[64,128]{1,0:T(8,128)(2,1)} %param.17) | copy-start | bytes 49156
  83.9 19.9 %collective-permute-start.2 = (bf16[2,64,11,256]{3,1,2,0:T(8,128)(2,1)}, bf16[2,64,11,256]{3,1,2,0:T(8,128)(2,1)}, u32[]{:S(2)}, u32[]{:S(2)}) collective-permute-start(bf16[2,64,11,256]{3,1,2,0:T(8,128)(2,1)} %copy.115), channel_id=1, source_target_pairs={{4,0},{8,4},{12,8},{16,12},{20,16},{24,20},{28,24},{32,28},{36,32}... | collective-permute-start | bytes 2162696 | tf_op jit(solution)/shard_map/ppermute | solution.py:31
  129.1 2.5 copy-start.7
  137.3 107.7 %all-to-all-start = ((bf16[32,2,2,64,144]{4,3,2,1,0:T(8,128)(2,1)}), bf16[32,2,2,64,144]{4,3,2,1,0:T(8,128)(2,1)}, u32[]{:S(2)}, u32[]{:S(2)}) async-start(bf16[32,2,2,64,144]{4,3,2,1,0:T(8,128)(2,1)} %scatter_fusion), calls=%async_computation | async-start | bytes 8388608 | tf_op jit(solution)/shard_map/all_to_all | solution.py:230
  152.9 687.9 %all-reduce.15.cloned.1.call-start = ((), (), s32[]{:S(2)}) async-start(), calls=%async_computation.1 | async-start | bytes 2359296 | tf_op jit(solution)/shard_map/psum | solution.py:240
  252.6 2.6 copy-start.8
  252.6 2.6 copy-start.10
  252.6 2.6 copy-start.11
  262.6 2.9 copy-start.2
  265.6 1.8 copy-start.3
  282.1 2.9 copy-start.2
  285.1 1.8 copy-start.3
  302.7 2.9 copy-start.2
  323.3 2.9 copy-start.2
  326.2 1.8 copy-start.3
  343.8 2.9 copy-start.2
  364.4 2.9 copy-start.2
  385.0 2.9 copy-start.2
  405.5 2.9 copy-start.2
  426.1 2.9 copy-start.2
  446.6 2.9 copy-start.2
  467.2 2.9 copy-start.2
  487.8 2.9 copy-start.2
  508.3 2.9 copy-start.2
  528.9 2.9 copy-start.2
  549.5 2.9 copy-start.2
  570.0 2.9 copy-start.2
  583.2 261.5 %copy-start.1 = (bf16[128,900]{0,1:T(8,128)(2,1)S(1)}, bf16[128,900]{0,1:T(8,128)(2,1)}, u32[]{:S(2)}) copy-start(bf16[128,900]{0,1:T(8,128)(2,1)} %param.16) | copy-start | bytes 691204
  (61 other events, 84.2 us)
Sparse Core Ops, SparseCore 0:
  583.3 257.4 all-reduce.14
where the time goes:
time: 859 us; the launch traced here: 851 us
  waiting for transfers between devices  279 us (32%)
  matrix products  190 us (22%)
  local copies, waits for them, and re-layouts  148 us (17%)
  other arithmetic  119 us (14%)
  blocking collectives  74.9 us (9%)
  starting transfers between devices  22 us (3%)
  between operations  14.3 us (2%)
    dot_general x129, matrix products, product(): return jnp.einsum(form, left, right, preferred_element_type=jnp.float32)  190 us
    psum x1, waiting for transfers between devices, per_device(): lax.psum((gradients[0], gradients[1], gradients[2], gradients[3]), ('segm...  181 us
    all_to_all x1, waiting for transfers between devices, per_device(): lax.all_to_all(outgoing, 'rows', split_axis=0, concat_axis=0, tiled=True)  81 us
    psum x1, blocking collectives, per_device(): lax.psum((gradients[0], gradients[1], gradients[2], gradients[3]), ('segm...  74.9 us
    concatenate x1, local copies, waits for them, and re-layouts, columns(): jnp.concatenate([shifted(values, row_step, col_step, stride) for row_step...  41.7 us
    while x256, other arithmetic  34.1 us
    another operation x19, other arithmetic  27.5 us
    dynamic_update_slice x16, local copies, waits for them, and re-layouts, run_blocks(): gradients, losses = lax.scan(advance, initial, stacked)  21.3 us
  transfers between devices with their start and end apart: 5, of which 4 were waited for; matrix products, arithmetic and copies ran while one was open for 2% of the time, Pallas kernels for 0%

commit v1 on v0

--- a/solution.py
+++ b/solution.py
@@ -238,7 +238,8 @@
     )
     owner_total = jnp.sum(losses)
     totals = lax.psum(
-        (gradients[0], gradients[1], gradients[2], gradients[3]), ("segment", "rows", "dp")
+        lax.psum((gradients[0], gradients[1], gradients[2], gradients[3]), "segment"),
+        ("rows", "dp"),
     )
     return (mean_strip[None], owner_total.reshape(1, 1), totals[0], totals[1], totals[2], totals[3])
 

time: 859 us -> 1310 us (1.53)
  blocking collectives: 74.9 us -> 686 us
  waiting for transfers between devices: 279 us -> 127 us
    psum x1 -> x2, blocking collectives: 74.9 us -> 686 us  [the longest x1 682 us: per_device(): lax.psum(lax.psum((gradients[0], gradients[1], gradients[2], gradients[3]...]
    psum x1 -> x2, waiting for transfers between devices: 181 us -> 29.2 us  [the longest x1 29.2 us: per_device(): lax.psum((gradients[0], gradients[1], gradients[2], gradients[3]), 'segme...]
    dynamic_update_slice x16, local copies, waits for them, and re-layouts: 21.3 us -> 0.61 us  [run_blocks(): gradients, losses = lax.scan(advance, initial, stacked)]
  transfers between devices with their start and end apart: 5 -> 6, of which waited for: 4 -> 4; matrix products, arithmetic and copies ran while one was open for 2% -> 1% of each run, Pallas kernels for 0% -> 0%
where the time goes in v1:
time: 1310 us; the launch traced here: 1300 us
  blocking collectives  686 us (52%)
  matrix products  190 us (15%)
  local copies, waits for them, and re-layouts  138 us (11%)
  waiting for transfers between devices  127 us (10%)
  other arithmetic  118 us (9%)
  starting transfers between devices  22 us (2%)
  between operations  14.3 us (1%)
    psum x1, blocking collectives, per_device(): lax.psum(lax.psum((gradients[0], gradients[1], gradients[2], gradients[3]...  682 us
    dot_general x129, matrix products, product(): return jnp.einsum(form, left, right, preferred_element_type=jnp.float32)  190 us
    all_to_all x1, waiting for transfers between devices, per_device(): lax.all_to_all(outgoing, 'rows', split_axis=0, concat_axis=0, tiled=True)  81 us
    concatenate x1, local copies, waits for them, and re-layouts, columns(): jnp.concatenate([shifted(values, row_step, col_step, stride) for row_step...  41.7 us
    while x256, other arithmetic  34.1 us
    psum x1, waiting for transfers between devices, per_device(): lax.psum((gradients[0], gradients[1], gradients[2], gradients[3]), 'segme...  29.2 us
    another operation x19, other arithmetic  27.5 us
  transfers between devices with their start and end apart: 6, of which 4 were waited for; matrix products, arithmetic and copies ran while one was open for 1% of the time, Pallas kernels for 0%

profile of v1, /device:TPU:8, one launch (start us, length us, event | category | flops | bytes accessed | tf_op | source)
XLA Modules:
  0.0 1299.1 jit_solution(337058999632106801)
XLA Ops:
  8.1 3.4 collective-permute-start
  12.8 3.2 copy.114
  18.2 4.4 slice_select_fusion.1
  22.6 41.7 %concatenate.38 = bf16[900,3584]{1,0:T(8,128)(2,1)} concatenate(bf16[100,3584]{1,0:T(8,128)(2,1)} %get-tuple-element.391, bf16[100,3584]{1,0:T(8,128)(2,1)} %get-tuple-element.394, bf16[100,3584]{1,0:T(8,128)(2,1)} %get-tuple-element.384, bf16[100,3584]{1,0:T(8,128)(2,1)} %get-tuple-element.392, bf16[100,3584]{1,0:T(8,128)(2,1)} %get-tuple-element.395, ...), dimensions={0} | concatenate | bytes 12902400 | tf_op jit(solution)/shard_map/concatenate | solution.py:47
  64.3 5.4 fusion.29
  71.2 3.2 copy.113
  74.4 4.9 pad_maximum_fusion.2
  79.3 4.6 copy.115
  87.4 16.4 %collective-permute-done.2 = bf16[2,64,11,256]{3,1,2,0:T(8,128)(2,1)} collective-permute-done((bf16[2,64,11,256]{3,1,2,0:T(8,128)(2,1)}, bf16[2,64,11,256]{3,1,2,0:T(8,128)(2,1)}, u32[]{:S(2)}, u32[]{:S(2)}) %collective-permute-start.2) | collective-permute-done | bytes 720928 | tf_op jit(solution)/shard_map/ppermute | solution.py:31
  103.8 4.7 copy.116
  108.4 8.1 pad_maximum_fusion.1
  116.5 8.6 gather_fusion
  125.2 3.9 copy.117
  131.6 5.7 scatter_fusion
  137.3 15.6 %all-to-all-start = ((bf16[32,2,2,64,144]{4,3,2,1,0:T(8,128)(2,1)}), bf16[32,2,2,64,144]{4,3,2,1,0:T(8,128)(2,1)}, u32[]{:S(2)}, u32[]{:S(2)}) async-start(bf16[32,2,2,64,144]{4,3,2,1,0:T(8,128)(2,1)} %scatter_fusion), calls=%async_computation | async-start | bytes 8388608 | tf_op jit(solution)/shard_map/all_to_all | solution.py:230
  153.4 9.0 reduce-window.6
  164.0 81.0 %all-to-all-done = bf16[32,2,2,64,144]{4,3,2,1,0:T(8,128)(2,1)} async-done(((bf16[32,2,2,64,144]{4,3,2,1,0:T(8,128)(2,1)}), bf16[32,2,2,64,144]{4,3,2,1,0:T(8,128)(2,1)}, u32[]{:S(2)}, u32[]{:S(2)}) %all-to-all-start) | async-done | bytes 2359328 | tf_op jit(solution)/shard_map/all_to_all | solution.py:230
  245.0 5.0 gather_fusion.1
  255.2 317.5 %while.21 = (s32[]{:T(128)}, f32[128,1152]{1,0:T(8,128)}, f32[128,1152]{1,0:T(8,128)}, f32[64,128]{1,0:T(8,128)S(1)}, f32[32,128]{1,0:T(8,128)S(1)}, /*index=5*/...) while((s32[]{:T(128)}, f32[128,1152]{1,0:T(8,128)}, ...), condition=%wide.region_15.16_spmd.clone, body=%wide.region_9.15_spmd.clone.sunk | while | flops 884677568 | bytes 48410204 | solution.py:159
  286.3 2.8 fusion.117
  306.2 2.8 fusion.117
  326.1 2.8 fusion.117
  346.0 2.8 fusion.117
  365.9 2.8 fusion.117
  385.8 2.8 fusion.117
  425.6 2.8 fusion.117
  445.5 2.8 fusion.117
  465.4 2.8 fusion.117
  485.3 2.8 fusion.117
  572.7 29.2 %all-reduce.20.cloned.1.call-done = (f32[128,1152]{1,0:T(8,128)}, f32[128,1152]{1,0:T(8,128)}) async-done(((f32[128,1152]{1,0:T(8,128)}, f32[128,1152]{1,0:T(8,128)}), (f32[128,1152]{1,0:T(8,128)}, f32[128,1152]{1,0:T(8,128)})) %all-reduce.20.cloned.1.call-update) | async-done | bytes 1179664 | tf_op jit(solution)/shard_map/psum | solution.py:241
  602.6 3.6 all-reduce.13
  606.2 682.2 %all-reduce.11 = (f32[64,128]{1,0:T(8,128)}, f32[32,128]{1,0:T(8,128)}) all-reduce(f32[64,128]{1,0:T(8,128)S(1)} %get-tuple-element.354, f32[32,128]{1,0:T(8,128)S(1)} %get-tuple-element.355), channel_id=1, replica_groups=mesh['segment'=2,'rows'=32,'dp'=4] {'rows','dp'}, use_global_device_ids=true, to_apply=%region_22.23 | all-reduce | flops 12288 | bytes 98304 | tf_op jit(solution)/shard_map/psum | solution.py:240
  (913 shorter events, 308.7 us)
Async XLA Ops:
  7.2 57.2 %copy-start = (bf16[128,900]{0,1:T(8,128)(2,1)S(1)}, bf16[128,900]{0,1:T(8,128)(2,1)}, u32[]{:S(2)}) copy-start(bf16[128,900]{0,1:T(8,128)(2,1)} %param.16) | copy-start | bytes 691204
  7.2 10.4 copy-start.9
  8.1 8.8 collective-permute-start
  11.5 6.0 collective-permute-start.1
  22.6 41.7 %copy-start.12 = (bf16[64,128]{1,0:T(8,128)(2,1)S(1)}, bf16[64,128]{1,0:T(8,128)(2,1)}, u32[]{:S(2)}) copy-start(bf16[64,128]{1,0:T(8,128)(2,1)} %param.17) | copy-start | bytes 49156
  83.9 19.9 %collective-permute-start.2 = (bf16[2,64,11,256]{3,1,2,0:T(8,128)(2,1)}, bf16[2,64,11,256]{3,1,2,0:T(8,128)(2,1)}, u32[]{:S(2)}, u32[]{:S(2)}) collective-permute-start(bf16[2,64,11,256]{3,1,2,0:T(8,128)(2,1)} %copy.115), channel_id=1, source_target_pairs={{4,0},{8,4},{12,8},{16,12},{20,16},{24,20},{28,24},{32,28},{36,32}... | collective-permute-start | bytes 2162696 | tf_op jit(solution)/shard_map/ppermute | solution.py:31
  129.1 2.5 copy-start.7
  137.3 107.7 %all-to-all-start = ((bf16[32,2,2,64,144]{4,3,2,1,0:T(8,128)(2,1)}), bf16[32,2,2,64,144]{4,3,2,1,0:T(8,128)(2,1)}, u32[]{:S(2)}, u32[]{:S(2)}) async-start(bf16[32,2,2,64,144]{4,3,2,1,0:T(8,128)(2,1)} %scatter_fusion), calls=%async_computation | async-start | bytes 8388608 | tf_op jit(solution)/shard_map/all_to_all | solution.py:230
  152.9 449.0 %all-reduce.20.cloned.1.call-start = ((), (), s32[]{:S(2)}) async-start(), calls=%async_computation.2 | async-start | bytes 2359296 | tf_op jit(solution)/shard_map/psum | solution.py:241
  252.6 2.6 copy-start.8
  252.6 2.6 copy-start.10
  252.6 2.6 copy-start.11
  262.6 2.9 copy-start.2
  281.5 2.9 copy-start.2
  284.4 1.8 copy-start.3
  301.4 2.9 copy-start.2
  304.3 1.8 copy-start.3
  321.3 2.9 copy-start.2
  341.2 2.9 copy-start.2
  361.1 2.9 copy-start.2
  381.0 2.9 copy-start.2
  400.9 2.9 copy-start.2
  420.8 2.9 copy-start.2
  440.7 2.9 copy-start.2
  460.7 2.9 copy-start.2
  480.6 2.9 copy-start.2
  500.5 2.9 copy-start.2
  520.4 2.9 copy-start.2
  540.3 2.9 copy-start.2
  560.2 2.9 copy-start.2
  572.6 719.6 %copy-start.1 = (bf16[128,900]{0,1:T(8,128)(2,1)S(1)}, bf16[128,900]{0,1:T(8,128)(2,1)}, u32[]{:S(2)}) copy-start(bf16[128,900]{0,1:T(8,128)(2,1)} %param.16) | copy-start | bytes 691204
  572.7 715.8 %all-reduce.18.cloned.1.call-start = ((), (), s32[]{:S(2)}) async-start(), calls=%async_computation.1 | async-start | bytes 2359296 | tf_op jit(solution)/shard_map/psum | solution.py:240
  (62 other events, 75.6 us)
Sparse Core Ops, SparseCore 0:
  572.8 29.1 all-reduce.19
  608.4 222.2 all-reduce.17
